TPU v7x, 32 devices: a whole 2x2x4 slice. The times are simulated.
32 devices in a mesh: img: 8 (over z, y), seq: 4 (over x, core).
Axes of the slice: x: 2, y: 2, z: 4, core: 2. Of those that a mesh axis runs over, the one named last changes fastest.
Arguments:
- tokens: bfloat16 [8, 512, 1152], P('img', 'seq'), may hold values from -6 to 6
- counts: int32 [8, 4], P('img'), may hold values from 96 to 128, as said below
- w_qkv: bfloat16 [3981312], P(('img', 'seq')), may hold values from -1 to 1
- w_out: bfloat16 [1327104], P(('img', 'seq')), may hold values from -1.5 to 1.5
- w_fc1: bfloat16 [4958208], P(('img', 'seq')), may hold values from -0.1875 to 0.1875
- w_fc2: bfloat16 [4958208], P(('img', 'seq')), may hold values from -0.09375 to 0.09375
- vectors: bfloat16 [13536], P(('img', 'seq')), may hold values from -2 to 2
- cotangent: bfloat16 [8, 512, 1152], P('img', 'seq'), may hold values from -6 to 6
Outputs:
- output: bfloat16 [8, 512, 1152], P('img', 'seq')
- input_grad: float32 [8, 512, 1152], P('img', 'seq')
- grad_qkv: float32 [3981312], P(('img', 'seq'))
- grad_out: float32 [1327104], P(('img', 'seq'))
- grad_fc1: float32 [4958208], P(('img', 'seq'))
- grad_fc2: float32 [4958208], P(('img', 'seq'))
- grad_vectors: float32 [11232], P(('img', 'seq'))
- grad_front: float32 [2304], P(('img', 'seq'))
Inputs may be any that keep to these rules, and one draw needn't show every extreme that they name: An image's counts come from one length L of 385 to 512 tokens: every slice gets L // 4 and the first L mod 4 slices one more; some image is full in every draw.
All inputs are finite; a program needn't handle non-finite values.
Results may differ from a plain program's by a relative error of at most 0.011.
Values may be sent and summed in bfloat16 or wider, within the bound.
A program may use at most 320 MiB of HBM per device.

v0:
```python
import jax
import jax.numpy as jnp
from jax import lax
from jax.sharding import PartitionSpec as P

HEADS = 16
HEAD_DIM = 72


EPS = 1e-06
GELU_C = 0.7978845608028654


def normalize(values):
    mean = jnp.mean(values, axis=-1, keepdims=True)
    centred = values - mean
    rstd = lax.rsqrt(jnp.mean(centred * centred, axis=-1, keepdims=True) + EPS)
    return (centred * rstd, rstd)


def norm_back(grad_in, normed, rstd, gain):
    scaled = grad_in * gain
    return rstd * (
        scaled
        - jnp.mean(scaled, axis=-1, keepdims=True)
        - normed * jnp.mean(scaled * normed, axis=-1, keepdims=True)
    )


def gelu_parts(pre):
    inner = GELU_C * (pre + 0.044715 * pre * pre * pre)
    tanh_v = jnp.tanh(inner)
    value = 0.5 * pre * (1.0 + tanh_v)
    slope = 0.5 * (1.0 + tanh_v) + 0.5 * pre * (1.0 - tanh_v * tanh_v) * GELU_C * (
        1.0 + 3.0 * 0.044715 * pre * pre
    )
    return (value, slope)


def split_heads(values):
    return values.reshape(values.shape[0], HEADS, HEAD_DIM)


def unpack(vec_flat, width, hidden):
    vec = vec_flat.astype(jnp.float32)
    parts = [vec[i * width : (i + 1) * width] for i in range(8)]
    parts.append(vec[8 * width : 8 * width + hidden])
    return parts


def masked_scores(queries, keys_all, key_valid):
    scale = HEAD_DIM ** (-0.5)
    scores = (
        jnp.einsum(
            "shd,thd->hst",
            split_heads(queries),
            split_heads(keys_all),
            preferred_element_type=jnp.float32,
        )
        * scale
    )
    return jnp.where(key_valid[None, None, :], scores, -1e30)


def flat_range(left, right):
    block = lax.dot_general(
        left, right, (((0,), (0,)), ((), ())), preferred_element_type=jnp.float32
    ).reshape(-1)
    return block


def shards(tokens, counts, w_qkv, w_out, w_fc1, w_fc2, vectors, cotangent):
    f32 = jnp.float32
    bf16 = jnp.bfloat16
    width = tokens.shape[2]
    slot = tokens.shape[1]
    scale = HEAD_DIM ** (-0.5)
    position = lax.axis_index("seq")
    seq_count = lax.axis_size("seq")
    device_count = lax.axis_size("img") * seq_count
    slice_counts = counts[0]
    key_valid = (jnp.arange(slot)[None, :] < slice_counts[:, None]).reshape(-1)
    row_valid = lax.dynamic_slice_in_dim(key_valid, position * slot, slot)
    rowmask = row_valid.astype(f32)[:, None]
    x = tokens[0].astype(f32)
    qkv_flat, out_flat, vec_flat = (
        lax.all_gather(w_qkv, ("img", "seq"), axis=0, tiled=True),
        lax.all_gather(w_out, ("img", "seq"), axis=0, tiled=True),
        lax.all_gather(vectors, ("img", "seq"), axis=0, tiled=True),
    )
    fc1_flat, fc2_flat = (
        lax.all_gather(w_fc1, ("img", "seq"), axis=0, tiled=True),
        lax.all_gather(w_fc2, ("img", "seq"), axis=0, tiled=True),
    )
    hidden = fc1_flat.shape[0] // width
    mat_qkv = qkv_flat.reshape(width, 3 * width)
    mat_out = out_flat.reshape(width, width)
    mat_fc1 = fc1_flat.reshape(width, hidden)
    mat_fc2 = fc2_flat.reshape(hidden, width)
    bias1, v_bias, gain1, q_bias, out_bias, gain2, bias2, fc2_bias, fc1_bias = unpack(
        vec_flat, width, hidden
    )
    normed1, rstd1 = normalize(x)
    ln1 = (normed1 * gain1 + bias1).astype(bf16)
    qkv = jnp.dot(ln1, mat_qkv, preferred_element_type=f32)
    queries = (qkv[:, :width] + q_bias).astype(bf16)
    keys = qkv[:, width : 2 * width].astype(bf16)
    values = (qkv[:, 2 * width :] + v_bias).astype(bf16)
    keys_all, values_all = (
        lax.all_gather(keys, "seq", axis=0, tiled=True),
        lax.all_gather(values, "seq", axis=0, tiled=True),
    )
    scores = masked_scores(queries, keys_all, key_valid)
    top = jnp.max(scores, axis=-1, keepdims=True)
    lse = top + jnp.log(jnp.sum(jnp.exp(scores - top), axis=-1, keepdims=True))
    probs = jnp.exp(scores - lse).astype(bf16)
    mixed = (
        jnp.einsum("hst,thd->shd", probs, split_heads(values_all), preferred_element_type=f32)
        .reshape(slot, width)
        .astype(bf16)
    )
    resid = x + jnp.dot(mixed, mat_out, preferred_element_type=f32) + out_bias
    normed2, rstd2 = normalize(resid)
    ln2 = (normed2 * gain2 + bias2).astype(bf16)
    pre = jnp.dot(ln2, mat_fc1, preferred_element_type=f32) + fc1_bias
    act_f, slope = gelu_parts(pre)
    act = act_f.astype(bf16)
    output = (
        (resid + jnp.dot(act, mat_fc2, preferred_element_type=f32) + fc2_bias) * rowmask
    ).astype(bf16)
    fc1_again, fc2_again = (
        lax.all_gather(w_fc1, ("img", "seq"), axis=0, tiled=True),
        lax.all_gather(w_fc2, ("img", "seq"), axis=0, tiled=True),
    )
    back_fc1 = fc1_again.reshape(width, hidden)
    back_fc2 = fc2_again.reshape(hidden, width)
    grad_y = cotangent[0].astype(f32) * rowmask
    grad_y16 = grad_y.astype(bf16)
    grad_act = jnp.dot(grad_y16, back_fc2.T, preferred_element_type=f32)
    grad_pre = grad_act * slope
    grad_pre16 = grad_pre.astype(bf16)
    grad_ln2 = jnp.dot(grad_pre16, back_fc1.T, preferred_element_type=f32)
    grad_resid = grad_y + norm_back(grad_ln2, normed2, rstd2, gain2)
    shard_fc1 = w_fc1.shape[0]
    shard_fc2 = w_fc2.shape[0]
    mlp_shard = shard_fc1 + shard_fc2
    blocks = mlp_shard * lax.axis_size(("img", "seq")) // mlp_shard
    part_fc1 = flat_range(ln2, grad_pre16).reshape(blocks, shard_fc1)
    part_fc2 = flat_range(act, grad_y16).reshape(blocks, shard_fc2)
    mlp_mine = lax.psum_scatter(
        jnp.concatenate([part_fc1, part_fc2], axis=1).reshape(-1),
        ("img", "seq"),
        scatter_dimension=0,
        tiled=True,
    )
    grad_fc1 = mlp_mine[:shard_fc1]
    grad_fc2 = mlp_mine[shard_fc1:]
    qkv_again, out_again, vec_again = (
        lax.all_gather(w_qkv, ("img", "seq"), axis=0, tiled=True),
        lax.all_gather(w_out, ("img", "seq"), axis=0, tiled=True),
        lax.all_gather(vectors, ("img", "seq"), axis=0, tiled=True),
    )
    back_qkv = qkv_again.reshape(width, 3 * width)
    back_out = out_again.reshape(width, width)
    back_gain1 = unpack(vec_again, width, hidden)[2]
    grad_resid16 = grad_resid.astype(bf16)
    grad_mixed16 = jnp.dot(grad_resid16, back_out.T, preferred_element_type=f32).astype(bf16)
    gm_heads = split_heads(grad_mixed16)
    delta = jnp.einsum("shd,shd->hs", gm_heads.astype(f32), split_heads(mixed).astype(f32))
    value_terms = jnp.einsum("hst,shd->thd", probs, gm_heads, preferred_element_type=f32).reshape(
        -1, width
    )
    dots = jnp.einsum("shd,thd->hst", gm_heads, split_heads(values_all), preferred_element_type=f32)
    grad_scores = (jnp.exp(scores - lse) * (dots - delta[:, :, None]) * scale).astype(bf16)
    grad_queries = jnp.einsum(
        "hst,thd->shd", grad_scores, split_heads(keys_all), preferred_element_type=f32
    ).reshape(slot, width)
    key_terms = jnp.einsum(
        "hst,shd->thd", grad_scores, split_heads(queries), preferred_element_type=f32
    ).reshape(-1, width)
    grad_keys, grad_values = (
        lax.psum_scatter(
            key_terms.astype(jnp.bfloat16), "seq", scatter_dimension=0, tiled=True
        ).astype(jnp.float32),
        lax.psum_scatter(
            value_terms.astype(jnp.bfloat16), "seq", scatter_dimension=0, tiled=True
        ).astype(jnp.float32),
    )
    grad_qkv16 = jnp.concatenate(
        [grad_queries.astype(bf16), grad_keys.astype(bf16), grad_values.astype(bf16)], axis=1
    )
    grad_ln1 = jnp.dot(grad_qkv16, back_qkv.T, preferred_element_type=f32)
    input_grad = grad_resid + norm_back(grad_ln1, normed1, rstd1, back_gain1)
    unused = vec_flat.shape[0] - 8 * width - hidden
    g_front = jnp.concatenate([jnp.sum(grad_ln1, axis=0), jnp.sum(grad_values, axis=0)])
    g_rest = jnp.concatenate(
        [
            jnp.sum(grad_ln1 * normed1, axis=0),
            jnp.sum(grad_queries, axis=0),
            jnp.sum(grad_resid, axis=0),
            jnp.sum(grad_ln2 * normed2, axis=0),
            jnp.sum(grad_ln2, axis=0),
            jnp.sum(grad_y, axis=0),
            jnp.sum(grad_pre, axis=0),
            jnp.zeros((unused,), f32),
        ]
    )
    shard_qkv = w_qkv.shape[0]
    shard_out = w_out.shape[0]
    shard_vec = vectors.shape[0]
    shard_front = 2 * width // device_count
    shard_rest = shard_vec - shard_front
    attn_shard = shard_qkv + shard_out + shard_vec
    blocks = attn_shard * lax.axis_size(("img", "seq")) // attn_shard
    part_qkv = flat_range(ln1, grad_qkv16).reshape(blocks, shard_qkv)
    part_out = flat_range(mixed, grad_resid16).reshape(blocks, shard_out)
    part_front = g_front.reshape(blocks, shard_front)
    part_rest = g_rest.reshape(blocks, shard_rest)
    attn_mine = lax.psum_scatter(
        jnp.concatenate([part_qkv, part_out, part_front, part_rest], axis=1).reshape(-1),
        ("img", "seq"),
        scatter_dimension=0,
        tiled=True,
    )
    grad_qkv = attn_mine[:shard_qkv]
    grad_out = attn_mine[shard_qkv : shard_qkv + shard_out]
    grad_front = attn_mine[shard_qkv + shard_out : shard_qkv + shard_out + shard_front]
    grad_vectors = attn_mine[shard_qkv + shard_out + shard_front :]
    return (
        output[None],
        input_grad[None],
        grad_qkv,
        grad_out,
        grad_fc1,
        grad_fc2,
        grad_vectors,
        grad_front,
    )


def solution(mesh):
    return jax.shard_map(
        shards,
        mesh=mesh,
        in_specs=(
            P("img", "seq", None),
            P("img", None),
            P(("img", "seq")),
            P(("img", "seq")),
            P(("img", "seq")),
            P(("img", "seq")),
            P(("img", "seq")),
            P("img", "seq", None),
        ),
        out_specs=(
            P("img", "seq", None),
            P("img", "seq", None),
            P(("img", "seq")),
            P(("img", "seq")),
            P(("img", "seq")),
            P(("img", "seq")),
            P(("img", "seq")),
            P(("img", "seq")),
        ),
        check_vma=False,
    )
```

profile of v0, /device:TPU:0, one launch (start us, length us, event | category | flops | bytes accessed | tf_op | source)
XLA Modules:
  0.0 1720.6 jit_solution(5734492980531281552)
XLA Ops:
  7.2 2.0 reshape.201
  11.0 4.2 broadcast.122.clone
  15.2 5.8 dynamic-update-slice.2
  21.0 4.3 broadcast.122.clone.1
  25.4 5.8 dynamic-update-slice.1
  32.0 44.6 %all-reduce = bf16[13536]{0:T(1024)(128)(2,1)S(1)} all-reduce(bf16[13536]{0:T(1024)(128)(2,1)S(1)} %dynamic-update-slice), channel_id=1, replica_groups=mesh['img'=8,'seq'=4] {'img','seq'}, use_global_device_ids=true, to_apply=%add | all-reduce | flops 13536 | bytes 54144
  77.6 47.8 %all-gather.11.cloned.1.call-done = bf16[32,1,124416]{2,1,0:T(2,128)(2,1)} async-done(((bf16[1,1,124416]{2,1,0:T(2,128)(2,1)}), bf16[32,1,124416]{2,1,0:T(2,128)(2,1)}) %all-gather.11.cloned.1.call-update) | async-done | bytes 7962640 | tf_op jit(solution)/shard_map/all_gather | solution.py:87
  125.4 167.2 %reduce.3 = bf16[32,124416]{1,0:T(8,128)(2,1)} reduce(bf16[32,1,124416]{2,1,0:T(2,128)(2,1)} %all-gather.11.cloned.1.call-done, bf16[]{:T(256)} %constant.64), dimensions={1}, to_apply=%all-gather.reduce_sub_computation | reduce | bytes 15925250 | tf_op jit(solution)/shard_map/all_gather | solution.py:87
  292.6 15.2 reshape.183
  307.9 4.7 fusion.47
  314.4 47.1 %reduce.4 = bf16[32,41472]{1,0:T(8,128)(2,1)S(1)} reduce(bf16[32,1,41472]{2,1,0:T(2,128)(2,1)} %all-gather.13.cloned.1.call-done, bf16[]{:T(256)} %constant.64), dimensions={1}, to_apply=%all-gather.1.reduce_sub_computation | reduce | bytes 5308418 | tf_op jit(solution)/shard_map/all_gather | solution.py:88
  361.6 4.9 reshape.187
  366.5 147.2 %all-reduce.12.cloned.1.call-done = (bf16[4958208]{0:T(1024)(128)(2,1)}, bf16[4958208]{0:T(1024)(128)(2,1)}) async-done(((bf16[4958208]{0:T(1024)(128)(2,1)}, bf16[4958208]{0:T(1024)(128)(2,1)}), (bf16[4958208]{0:T(1024)(128)(2,1)}, bf16[4958208]{0:T(1024)(128)(2,1)})) %all-reduce.12.cloned.1.call-update) | async-done | bytes 19832848
  513.7 19.3 %reshape.189 = bf16[4304,1152]{1,0:T(8,128)(2,1)} reshape(bf16[4958208]{0:T(1024)(128)(2,1)} %get-tuple-element.18) | data formatting | bytes 19832832 | tf_op jit(solution)/shard_map/reshape | solution.py:99
  533.0 20.1 %reshape.188 = bf16[1152,4304]{1,0:T(8,128)(2,1)} reshape(bf16[4958208]{0:T(1024)(128)(2,1)} %get-tuple-element.19) | data formatting | bytes 19832832 | tf_op jit(solution)/shard_map/reshape | solution.py:98
  553.4 1.7 copy.31
  556.1 2.1 copy-done
  561.2 3.8 convolution_convert_fusion.3
  566.0 7.5 convolution_add_fusion
  573.5 7.7 fusion.82
  581.3 3.5 multiply_reduce_fusion
  587.5 1.8 copy.32
  589.4 4.5 convolution_convert_fusion.1
  593.9 2.4 copy.45
  597.4 4.4 multiply_convert_fusion
  604.6 2.7 copy.43
  607.3 9.6 fusion.51
  616.9 28.2 %reshape_reshape.15 = f32[32,154944]{1,0:T(8,128)} reshape(f32[4304,1152]{1,0:T(8,128)} %fusion.51) | data formatting | bytes 39665664 | tf_op jit(solution)/shard_map/reshape;reshape | solution.py:149
  645.1 11.0 fusion.40
  656.0 36.9 %reshape_reshape.14 = f32[32,154944]{1,0:T(8,128)} reshape(f32[1152,4304]{1,0:T(8,128)} %fusion.40) | data formatting | bytes 39665664 | tf_op jit(solution)/shard_map/reshape;reshape | solution.py:148
  693.0 27.5 %pad_maximum_fusion = f32[32,309888]{1,0:T(8,128)} fusion(f32[32,154944]{1,0:T(8,128)} %reshape_reshape.15, f32[32,154944]{1,0:T(8,128)} %reshape_reshape.14), kind=kLoop, calls=%fused_computation | loop fusion | flops 9916416 | bytes 79331328 | tf_op jit(solution)/shard_map/concatenate | solution.py:151
  720.6 3.2 fusion.64
  723.8 5.9 reshape_reshape.13
  729.7 3.5 fusion.79
  733.3 32.9 %reshape.193 = f32[9916416]{0:T(1024)} reshape(f32[32,309888]{1,0:T(8,128)} %pad_maximum_fusion) | data formatting | bytes 79331328 | tf_op jit(solution)/shard_map/reshape | solution.py:151
  767.4 1.8 copy.44
  769.2 6.9 fusion.26
  776.1 8.0 fusion.44
  784.3 12.5 reshape_reshape.12
  796.8 10.9 constant_dynamic-update-slice_fusion.1
  808.1 5.3 constant_dynamic-update-slice_fusion
  814.8 1.8 dynamic-update-slice.6
  816.6 27.9 %reshape.192 = f32[5321952]{0:T(1024)} reshape(f32[32,166311]{1,0:T(8,128)} %dynamic-update-slice.6) | data formatting | bytes 42575616 | tf_op jit(solution)/shard_map/reshape | solution.py:220
  845.2 6.7 fusion.6
  853.0 851.4 %all-reduce.10.cloned.1.call-done = (f32[5321952]{0:T(1024)}, f32[9916416]{0:T(1024)}) async-done(((f32[5321952]{0:T(1024)}, f32[9916416]{0:T(1024)}), (f32[5321952]{0:T(1024)}, f32[9916416]{0:T(1024)})) %all-reduce.10.cloned.1.call-update) | async-done | bytes 60953488
  1704.3 2.0 dynamic-slice.2
  1706.3 1.7 dynamic-slice.3
  1710.7 2.7 fusion.78
  (111 shorter events, 25.0 us)
Async XLA Ops:
  7.2 118.2 %all-gather.11.cloned.1.call-start = ((), (), s32[]{:S(2)}) async-start(), calls=%async_computation.4 | async-start | bytes 16422912 | tf_op jit(solution)/shard_map/all_gather | solution.py:87
  9.2 305.2 %all-gather.13.cloned.1.call-start = ((), (), s32[]{:S(2)}) async-start(), calls=%async_computation.5 | async-start | bytes 5474304 | tf_op jit(solution)/shard_map/all_gather | solution.py:88
  10.9 502.8 %all-reduce.12.cloned.1.call-start = ((), (), s32[]{:S(2)}) async-start(), calls=%async_computation.9 | async-start | bytes 39665664
  11.0 4.2 copy-start.16
  21.0 4.3 copy-start.17
  31.2 0.7 copy-start.19
  31.2 45.5 %copy-start.2 = (bf16[1,128,1152]{2,1,0:T(8,128)(2,1)S(1)}, bf16[1,128,1152]{2,1,0:T(8,128)(2,1)}, u32[]{:S(2)}) copy-start(bf16[1,128,1152]{2,1,0:T(8,128)(2,1)} %param.8) | copy-start | bytes 884740
  31.2 522.2 %all-gather.9.cloned.1.call-start = ((), (), s32[]{:S(2)}) async-start(), calls=%async_computation.3 | async-start | bytes 1474560 | tf_op jit(solution)/shard_map/all_gather | solution.py:110
  312.6 1.7 copy-start.20
  313.3 246.2 %all-gather.7.cloned.1.call-start = ((), (), s32[]{:S(2)}) async-start(), calls=%async_computation.2 | async-start | bytes 1474560 | tf_op jit(solution)/shard_map/all_gather | solution.py:111
  314.2 451.9 %reduce-scatter.9.cloned.1.call-start = ((), (), s32[]{:S(2)}) async-start(), calls=%async_computation.7 | async-start | bytes 1474560
  553.4 2.6 copy-start.9
  555.1 1.0 copy-start.3
  556.1 2.1 copy-start
  561.2 3.8 copy-start.11
  561.2 3.8 copy-start.1
  566.0 7.5 copy-start.12
  566.0 15.2 slice-start
  566.0 15.2 slice-start.1
  573.5 7.7 slice-start.2
  581.2 3.5 copy-start.8
  585.1 0.8 copy-start.4
  596.3 171.0 %reduce-scatter.7.cloned.1.call-start = ((), (), s32[]{:S(2)}) async-start(), calls=%async_computation.6 | async-start | bytes 1474560
  597.4 5.7 copy-start.10
  601.8 1.3 copy-start.7
  693.0 1011.3 %all-reduce.10.cloned.1.call-start = ((), (), s32[]{:S(2)}) async-start(), calls=%async_computation.8 | async-start | bytes 121913344
  693.0 27.5 %copy-start.5 = (f32[128,1152]{1,0:T(8,128)S(1)}, f32[128,1152]{1,0:T(8,128)}, u32[]{:S(2)}) copy-start(f32[128,1152]{1,0:T(8,128)} %copy-done.4) | copy-start | bytes 1769476
  769.2 6.9 copy-start.13
  769.2 6.9 copy-start.14
  844.5 0.7 copy-start.18
  845.2 6.7 copy-start.6
  845.2 6.7 copy-start.15
Sparse Core Ops, SparseCore 0:
  11.5 113.8 all-gather.10
  128.9 63.8 all-gather.12
  199.2 314.4 all-reduce.11
  515.7 17.2 all-gather.8
  535.0 17.4 all-gather.6
  596.4 25.3 reduce-scatter.8
  693.1 25.4 reduce-scatter.6
  844.6 859.6 all-reduce.9
where the time goes:
time: 1730 us; the launch traced here: 1720 us
  waiting for transfers between devices  1050 us (61%)
  local copies, waits for them, and re-layouts  277 us (16%)
  other arithmetic  247 us (14%)
  matrix products  89.6 us (5%)
  blocking collectives  44.6 us (3%)
    unnamed x12, waiting for transfers between devices  999 us
    all_gather x1, other arithmetic, shards(): lax.all_gather(w_qkv, ('img', 'seq'), axis=0, tiled=True)  167 us
    unnamed x63, local copies, waits for them, and re-layouts  55.3 us
    all_gather x1, waiting for transfers between devices, shards(): lax.all_gather(w_qkv, ('img', 'seq'), axis=0, tiled=True)  47.8 us
    all_gather x1, other arithmetic, shards(): lax.all_gather(w_out, ('img', 'seq'), axis=0, tiled=True)  47.1 us
    unnamed x1, blocking collectives  44.6 us
    another operation x1, local copies, waits for them, and re-layouts, shards(): part_fc1 = flat_range(ln2, grad_pre16).reshape(blocks, shard_fc1)  36.9 us
  transfers between devices with their start and end apart: 8, of which 3 were waited for; matrix products, arithmetic and copies ran while one was open for 28% of the time, Pallas kernels for 0%

commit v1 on v0

v1 whole, which is shorter than its diff:
```python
import jax
import jax.numpy as jnp
from jax import lax
from jax.sharding import PartitionSpec as P

HEADS = 16
HEAD_DIM = 72


EPS = 1e-06
GELU_C = 0.7978845608028654


def normalize(values):
    mean = jnp.mean(values, axis=-1, keepdims=True)
    centred = values - mean
    rstd = lax.rsqrt(jnp.mean(centred * centred, axis=-1, keepdims=True) + EPS)
    return (centred * rstd, rstd)


def norm_back(grad_in, normed, rstd, gain):
    scaled = grad_in * gain
    return rstd * (
        scaled
        - jnp.mean(scaled, axis=-1, keepdims=True)
        - normed * jnp.mean(scaled * normed, axis=-1, keepdims=True)
    )


def gelu_parts(pre):
    inner = GELU_C * (pre + 0.044715 * pre * pre * pre)
    tanh_v = jnp.tanh(inner)
    value = 0.5 * pre * (1.0 + tanh_v)
    slope = 0.5 * (1.0 + tanh_v) + 0.5 * pre * (1.0 - tanh_v * tanh_v) * GELU_C * (
        1.0 + 3.0 * 0.044715 * pre * pre
    )
    return (value, slope)


TILE = 2048
LANES = 128


def round_up(value, step):
    return -(-value // step) * step


def pack(flat):
    padded = round_up(flat.shape[0], TILE)
    return jnp.pad(flat, (0, padded - flat.shape[0])).reshape(-1, LANES)


def unpack_blocks(packed, blocks, length):
    return packed.reshape(blocks, -1)[:, :length].reshape(-1)


def pack_blocks(flat, blocks):
    block = flat.reshape(blocks, -1)
    padded = round_up(block.shape[1], TILE)
    return jnp.pad(block, ((0, 0), (0, padded - block.shape[1]))).reshape(-1, LANES)


def gather(value, axes):
    return lax.all_gather(value, axes, axis=0, tiled=True)


def scatter_sum(value, axes):
    return lax.psum_scatter(value, axes, scatter_dimension=0, tiled=True)


def weight_grad(left, right):
    return lax.dot_general(
        left, right, (((0,), (0,)), ((), ())), preferred_element_type=jnp.float32
    ).astype(jnp.bfloat16)


def dot_t(left, right):
    return lax.dot_general(
        left, right, (((1,), (1,)), ((), ())), preferred_element_type=jnp.float32
    )


def batched(left, right, over_left, over_right):
    return lax.dot_general(
        left,
        right,
        (((over_left,), (over_right,)), ((0,), (0,))),
        preferred_element_type=jnp.float32,
    )


def shards(tokens, counts, w_qkv, w_out, w_fc1, w_fc2, vectors, cotangent):
    f32 = jnp.float32
    bf16 = jnp.bfloat16
    width = tokens.shape[2]
    slot = tokens.shape[1]
    scale = HEAD_DIM ** (-0.5)
    position = lax.axis_index("seq")
    seq_count = lax.axis_size("seq")
    img_count = lax.axis_size("img")
    device_count = img_count * seq_count
    both = ("img", "seq")
    shard_qkv, shard_out, shard_fc1, shard_fc2, shard_vec = (
        w.shape[0] for w in (w_qkv, w_out, w_fc1, w_fc2, vectors)
    )
    hidden = shard_fc1 * device_count // width
    heads = HEADS // seq_count
    cols = width // seq_count
    units = hidden // seq_count
    rows = width // img_count
    pad_cols = round_up(3 * cols, LANES) - 3 * cols
    pad_units = round_up(units, LANES) - units
    to_quarter = [(c, (c % img_count) * seq_count + c // img_count) for c in range(device_count)]
    to_owner = [(b, a) for a, b in to_quarter]

    slice_counts = counts[0]
    key_valid = (jnp.arange(slot)[None, :] < slice_counts[:, None]).reshape(-1)
    row_valid = lax.dynamic_slice_in_dim(key_valid, position * slot, slot)
    rowmask = row_valid.astype(f32)[:, None]

    def mine(values):
        return lax.dynamic_slice_in_dim(values, position * slot, slot)

    qkv_seq = unpack_blocks(gather(pack(w_qkv), "seq"), seq_count, shard_qkv)
    out_vec = gather(pack(jnp.concatenate([w_out, vectors])), both)
    x_all16 = gather(tokens[0], "seq")
    qkv_rows = qkv_seq.reshape(rows, 3 * width)
    qkv_part = jnp.concatenate(
        [
            lax.dynamic_slice_in_dim(qkv_rows, j * width + position * cols, cols, axis=1)
            for j in range(3)
        ]
        + [jnp.zeros((rows, pad_cols), bf16)],
        axis=1,
    )
    mat_qkv = gather(qkv_part, "img")
    fc1_seq = unpack_blocks(gather(pack(w_fc1), "seq"), seq_count, shard_fc1)
    fc1_part = jnp.pad(
        lax.dynamic_slice_in_dim(
            fc1_seq.reshape(rows, hidden), position * units, units, axis=1
        ),
        ((0, 0), (0, pad_units)),
    )
    mat_fc1 = gather(fc1_part, "img")
    fc2_chunk = lax.ppermute(pack(w_fc2), both, to_quarter)
    mat_fc2 = jnp.pad(
        unpack_blocks(gather(fc2_chunk, "img"), img_count, shard_fc2).reshape(units, width),
        ((0, pad_units), (0, 0)),
    )
    cot_all = gather(cotangent[0], "seq")

    blocks_ov = out_vec.reshape(device_count, -1)
    mat_out = blocks_ov[:, :shard_out].reshape(width, width)
    vec = blocks_ov[:, shard_out : shard_out + shard_vec].reshape(-1).astype(f32)
    bias1, v_bias, gain1, q_bias, out_bias, gain2, bias2, fc2_bias = (
        vec[i * width : (i + 1) * width] for i in range(8)
    )
    fc1_bias = vec[8 * width : 8 * width + hidden]

    def my_cols(values):
        return lax.dynamic_slice_in_dim(values, position * cols, cols)

    fc1_bias_mine = jnp.pad(
        lax.dynamic_slice_in_dim(fc1_bias, position * units, units), (0, pad_units)
    )

    x = x_all16.astype(f32)
    normed1, _ = normalize(x)
    ln1 = (normed1 * gain1 + bias1).astype(bf16)
    qkv = jnp.dot(ln1, mat_qkv, preferred_element_type=f32)

    def by_head(values):
        return values.reshape(-1, heads, HEAD_DIM).transpose(1, 0, 2)

    def by_slot(values):
        return values.transpose(1, 0, 2).reshape(-1, cols)

    queries = by_head((qkv[:, :cols] + my_cols(q_bias)).astype(bf16))
    keys = by_head(qkv[:, cols : 2 * cols].astype(bf16))
    values = by_head((qkv[:, 2 * cols : 3 * cols] + my_cols(v_bias)).astype(bf16))
    scores = batched(queries, keys, 2, 2) * scale
    scores = jnp.where(key_valid[None, None, :], scores, -1e30)
    top = jnp.max(scores, axis=-1, keepdims=True)
    lse = top + jnp.log(jnp.sum(jnp.exp(scores - top), axis=-1, keepdims=True))
    probs = jnp.exp(scores - lse).astype(bf16)
    mixed_heads = batched(probs, values, 2, 1)
    mixed_mine = by_slot(mixed_heads).astype(bf16)
    mixed = lax.all_gather(mixed_mine, "seq", axis=0, tiled=True)
    mixed = (
        mixed.reshape(seq_count, -1, cols).transpose(1, 0, 2).reshape(-1, width)
    )
    resid = x + jnp.dot(mixed, mat_out, preferred_element_type=f32) + out_bias
    normed2, rstd2 = normalize(resid)
    ln2 = (normed2 * gain2 + bias2).astype(bf16)
    pre = jnp.dot(ln2, mat_fc1, preferred_element_type=f32) + fc1_bias_mine
    act_f, slope = gelu_parts(pre)
    act = act_f.astype(bf16)

    grad_y16 = jnp.where(key_valid[:, None], cot_all, jnp.zeros((), bf16))
    grad_pre = dot_t(grad_y16, mat_fc2) * slope
    grad_pre16 = grad_pre.astype(bf16)
    grad_ln2 = scatter_sum(dot_t(grad_pre16, mat_fc1).astype(bf16), "seq").astype(f32)
    grad_y = cotangent[0].astype(f32) * rowmask
    normed2_mine = mine(normed2)
    grad_resid = grad_y + norm_back(grad_ln2, normed2_mine, mine(rstd2), gain2)
    grad_resid16 = gather(grad_resid.astype(bf16), "seq")

    def reduce_rows(partial):
        return scatter_sum(partial, "img")

    sum_fc1 = reduce_rows(weight_grad(ln2, grad_pre16))
    sum_fc2 = reduce_rows(
        pack_blocks(weight_grad(act, grad_y16)[:units].reshape(-1), img_count)
    )
    out_terms = scatter_sum(
        jnp.dot(act, mat_fc2, preferred_element_type=f32).astype(bf16), "seq"
    ).astype(f32)
    output = ((mine(resid) + out_terms + fc2_bias) * rowmask).astype(bf16)

    out_mine = lax.dynamic_slice_in_dim(mat_out, position * cols, cols)
    gm = by_head(dot_t(grad_resid16, out_mine).astype(bf16))
    mixed_back = by_head(mixed_mine)
    delta = jnp.sum(gm.astype(f32) * mixed_back.astype(f32), axis=-1, keepdims=True)
    grad_values = by_slot(batched(probs, gm, 1, 1))
    dots = batched(gm, values, 2, 2)
    grad_scores = (jnp.exp(scores - lse) * (dots - delta) * scale).astype(bf16)
    grad_queries = by_slot(batched(grad_scores, keys, 2, 1))
    grad_keys = by_slot(batched(grad_scores, queries, 1, 1))
    grad_qkv16 = jnp.concatenate(
        [grad_queries.astype(bf16), grad_keys.astype(bf16), grad_values.astype(bf16)]
        + [jnp.zeros((seq_count * slot, pad_cols), bf16)],
        axis=1,
    )
    grad_ln1 = scatter_sum(dot_t(grad_qkv16, mat_qkv).astype(bf16), "seq").astype(f32)
    sum_qkv = reduce_rows(weight_grad(ln1, grad_qkv16))
    sum_out = reduce_rows(
        pack_blocks(weight_grad(mixed_mine, grad_resid16).reshape(-1), img_count)
    )
    normed1_mine, rstd1_mine = normalize(tokens[0].astype(f32))
    input_grad = grad_resid + norm_back(grad_ln1, normed1_mine, rstd1_mine, gain1)

    def own_block(rows_sum, thirds, used, size):
        blocks = gather(rows_sum, "seq").reshape(seq_count, rows, -1)[:, :, : thirds * used]
        whole = blocks.reshape(seq_count, rows, thirds, used).transpose(1, 2, 0, 3)
        return lax.dynamic_slice_in_dim(whole.reshape(-1), position * size, size).astype(f32)

    def own_chunk(packed, size):
        return lax.ppermute(packed, both, to_owner).reshape(-1)[:size].astype(f32)

    grad_fc1 = own_block(sum_fc1, 1, units, shard_fc1)
    grad_fc2 = own_chunk(sum_fc2, shard_fc2)
    grad_qkv = own_block(sum_qkv, 3, cols, shard_qkv)
    grad_out = own_chunk(sum_out, shard_out)

    def spread(part, full):
        return lax.dynamic_update_slice_in_dim(
            jnp.zeros((full,), f32), part, position * part.shape[0], 0
        )

    shard_front = 2 * width // device_count
    unused = shard_vec * device_count - 8 * width - hidden
    g_front = jnp.concatenate(
        [jnp.sum(grad_ln1, axis=0), spread(jnp.sum(grad_values, axis=0), width)]
    )
    g_rest = jnp.concatenate(
        [
            jnp.sum(grad_ln1 * normed1_mine, axis=0),
            spread(jnp.sum(grad_queries, axis=0), width),
            jnp.sum(grad_resid, axis=0),
            jnp.sum(grad_ln2 * normed2_mine, axis=0),
            jnp.sum(grad_ln2, axis=0),
            jnp.sum(grad_y, axis=0),
            spread(jnp.sum(grad_pre, axis=0)[:units], hidden),
            jnp.zeros((unused,), f32),
        ]
    )
    g_vec = jnp.concatenate(
        [g_front.reshape(device_count, -1), g_rest.reshape(device_count, -1)], axis=1
    )
    g_vec = jnp.pad(g_vec, ((0, 0), (0, round_up(shard_vec, 1024) - shard_vec)))
    vec_mine = scatter_sum(g_vec.reshape(-1, LANES), both).reshape(-1)
    return (
        output[None],
        input_grad[None],
        grad_qkv,
        grad_out,
        grad_fc1,
        grad_fc2,
        vec_mine[shard_front:shard_vec],
        vec_mine[:shard_front],
    )


def solution(mesh):
    return jax.shard_map(
        shards,
        mesh=mesh,
        in_specs=(
            P("img", "seq", None),
            P("img", None),
            P(("img", "seq")),
            P(("img", "seq")),
            P(("img", "seq")),
            P(("img", "seq")),
            P(("img", "seq")),
            P("img", "seq", None),
        ),
        out_specs=(
            P("img", "seq", None),
            P("img", "seq", None),
            P(("img", "seq")),
            P(("img", "seq")),
            P(("img", "seq")),
            P(("img", "seq")),
            P(("img", "seq")),
            P(("img", "seq")),
        ),
        check_vma=False,
    )
```

time: 1730 us -> 897 us (0.52)
  waiting for transfers between devices: 1050 us -> 657 us
  other arithmetic: 247 us -> 25.4 us
  local copies, waits for them, and re-layouts: 277 us -> 108 us
  matrix products: 89.6 us -> 55.3 us
  blocking collectives: 44.6 us -> 21.3 us
    unnamed x12 -> x19, waiting for transfers between devices: 999 us -> 126 us
    reduce_scatter x0 -> x7, waiting for transfers between devices: none -> 303 us  [scatter_sum(): return lax.psum_scatter(value, axes, scatter_dimension=0, tiled=True)]
    all_gather x2 -> x0, other arithmetic: 214 us -> none  [the longest x1 167 us: shards(): lax.all_gather(w_qkv, ('img', 'seq'), axis=0, tiled=True)]
    all_gather x4 -> x10, waiting for transfers between devices: 47.8 us -> 228 us  [the longest x9 228 us: gather(): return lax.all_gather(value, axes, axis=0, tiled=True)]
    reshape x7 -> x17, local copies, waits for them, and re-layouts: 121 us -> 34.9 us  [the longest x3 7.41 us: unpack_blocks(): return packed.reshape(blocks, -1)[:, :length].reshape(-1)]
    another operation x5 -> x9, local copies, waits for them, and re-layouts: 83.5 us -> 17.8 us  [the longest x2 6.08 us: pack_blocks(): block = flat.reshape(blocks, -1)]
    unnamed x1 -> x0, blocking collectives: 44.6 us -> none
    dot_general x16, matrix products: 84.2 us -> 47.9 us  [the longest x4 14 us: dot_t(): lax.dot_general(left, right, (((1,), (1,)), ((), ())), preferred_element_...]
  transfers between devices with their start and end apart: 8 -> 21, of which waited for: 3 -> 15; matrix products, arithmetic and copies ran while one was open for 28% -> 17% of each run, Pallas kernels for 0% -> 0%
where the time goes in v1:
time: 897 us; the launch traced here: 888 us
  waiting for transfers between devices  657 us (73%)
  local copies, waits for them, and re-layouts  108 us (12%)
  matrix products  55.3 us (6%)
  other arithmetic  25.4 us (3%)
  blocking collectives  21.3 us (2%)
  between operations  15.6 us (2%)
    reduce_scatter x7, waiting for transfers between devices, scatter_sum(): return lax.psum_scatter(value, axes, scatter_dimension=0, tiled=True)  303 us
    all_gather x9, waiting for transfers between devices, gather(): return lax.all_gather(value, axes, axis=0, tiled=True)  228 us
    unnamed x19, waiting for transfers between devices  126 us
    unnamed x118, local copies, waits for them, and re-layouts  29.4 us
    all_gather x2, blocking collectives, gather(): return lax.all_gather(value, axes, axis=0, tiled=True)  21.3 us
  transfers between devices with their start and end apart: 21, of which 15 were waited for; matrix products, arithmetic and copies ran while one was open for 17% of the time, Pallas kernels for 0%

profile of v1, /device:TPU:0, one launch (start us, length us, event | category | flops | bytes accessed | tf_op | source)
XLA Modules:
  0.0 887.9 jit_solution(10107417185913113270)
XLA Ops:
  10.6 11.2 %all_gather.38 = bf16[3904,128]{1,0:T(8,128)(2,1)S(1)} all-gather(bf16[976,128]{1,0:T(8,128)(2,1)S(1)} %pad_bitcast_fusion.2), channel_id=1, replica_groups=mesh['img'=8,'seq'=4] {'seq'}, dimensions={0}, use_global_device_ids=true | all-gather | bytes 1249280 | tf_op jit(solution)/shard_map/all_gather | solution.py:64
  27.3 2.4 all-gather.29.cloned.1.call-done
  33.0 59.2 %all-gather.13.cloned.1.call-done = bf16[10752,128]{1,0:T(8,128)(2,1)} async-done(((bf16[336,128]{1,0:T(8,128)(2,1)}), bf16[10752,128]{1,0:T(8,128)(2,1)}) %all-gather.13.cloned.1.call-update) | async-done | bytes 2752528 | tf_op jit(solution)/shard_map/all_gather | solution.py:64
  92.1 3.2 reshape.237
  96.1 46.5 %all-gather.15.cloned.1.call-done = bf16[1152,896]{1,0:T(8,128)(2,1)} async-done(((bf16[144,896]{1,0:T(8,128)(2,1)}), bf16[1152,896]{1,0:T(8,128)(2,1)}) %all-gather.15.cloned.1.call-update) | async-done | bytes 2064400 | tf_op jit(solution)/shard_map/all_gather | solution.py:64
  142.6 3.5 fusion.56
  148.2 2.2 copy.72
  156.2 2.2 fusion.5
  164.0 2.9 reshape.247
  166.9 2.4 slice.115
  169.3 4.0 reshape.272
  173.3 3.9 reshape_reshape.16
  179.9 36.2 %all-gather.23.cloned.1.call-done = bf16[9728,128]{1,0:T(8,128)(2,1)} async-done(((bf16[1216,128]{1,0:T(8,128)(2,1)}), bf16[9728,128]{1,0:T(8,128)(2,1)}) %all-gather.23.cloned.1.call-update) | async-done | bytes 2490384 | tf_op jit(solution)/shard_map/all_gather | solution.py:64
  216.1 4.2 reshape.249
  220.3 2.9 slice.117
  223.1 5.8 reshape.270
  228.9 5.9 reshape_reshape.17
  236.5 6.4 reshape.245
  243.6 3.5 reshape.243
  247.4 3.8 fusion.64
  253.8 38.0 %all-gather.21.cloned.1.call-done = bf16[1152,1152]{1,0:T(8,128)(2,1)} async-done(((bf16[144,1152]{1,0:T(8,128)(2,1)}), bf16[1152,1152]{1,0:T(8,128)(2,1)}) %all-gather.21.cloned.1.call-update) | async-done | bytes 2654224 | tf_op jit(solution)/shard_map/all_gather | solution.py:64
  291.9 5.7 convolution_add_fusion
  297.5 11.9 %all-gather.31.cloned.1.call-done = bf16[1,512,1152]{2,1,0:T(8,128)(2,1)} async-done(((bf16[1,128,1152]{2,1,0:T(8,128)(2,1)}), bf16[1,512,1152]{2,1,0:T(8,128)(2,1)}) %all-gather.31.cloned.1.call-update) | async-done | bytes 1179664 | tf_op jit(solution)/shard_map/all_gather | solution.py:64
  309.5 6.1 fusion.65
  316.6 3.0 convolution_convert_fusion.3
  319.7 5.6 convolution_convert_fusion.4
  327.9 17.5 %reduce-scatter.10.cloned.1.call-done = bf16[128,1152]{1,0:T(8,128)(2,1)} async-done(((bf16[512,1152]{1,0:T(8,128)(2,1)}), bf16[128,1152]{1,0:T(8,128)(2,1)}) %reduce-scatter.10.cloned.1.call-update) | async-done | bytes 294928 | tf_op jit(solution)/shard_map/reduce_scatter | solution.py:68
  347.9 25.6 %reduce-scatter.8.cloned.1.call-done = bf16[128,1152]{1,0:T(8,128)(2,1)} async-done(((bf16[512,1152]{1,0:T(8,128)(2,1)}), bf16[128,1152]{1,0:T(8,128)(2,1)}) %reduce-scatter.8.cloned.1.call-update) | async-done | bytes 294928 | tf_op jit(solution)/shard_map/reduce_scatter | solution.py:68
  373.5 3.0 fusion.58
  378.3 17.4 %all-gather.25.cloned.1.call-done = bf16[512,1152]{1,0:T(8,128)(2,1)} async-done(((bf16[128,1152]{1,0:T(8,128)(2,1)}), bf16[512,1152]{1,0:T(8,128)(2,1)}) %all-gather.25.cloned.1.call-update) | async-done | bytes 1179664 | tf_op jit(solution)/shard_map/all_gather | solution.py:64
  395.7 2.0 convolution_convert_fusion.6
  397.9 3.9 multiply_convert_fusion
  405.8 2.9 convolution_convert_fusion.2
  408.8 4.5 convolution_convert_fusion
  414.8 3.9 fusion.43
  420.4 5.8 reshape.274
  426.1 5.0 reshape_reshape.19
  431.1 3.3 pad.47
  434.4 4.3 reshape.258
  446.9 63.1 %reduce-scatter.18.cloned.1.call-done = bf16[144,1152]{1,0:T(8,128)(2,1)} async-done(((bf16[1152,1152]{1,0:T(8,128)(2,1)}), bf16[144,1152]{1,0:T(8,128)(2,1)}) %reduce-scatter.18.cloned.1.call-update) | async-done | bytes 331792 | tf_op jit(solution)/shard_map/reduce_scatter | solution.py:68
  510.1 72.8 %reduce-scatter.20.cloned.1.call-done = bf16[1216,128]{1,0:T(8,128)(2,1)} async-done(((bf16[9728,128]{1,0:T(8,128)(2,1)}), bf16[1216,128]{1,0:T(8,128)(2,1)}) %reduce-scatter.20.cloned.1.call-update) | async-done | bytes 311312 | tf_op jit(solution)/shard_map/reduce_scatter | solution.py:68
  584.8 3.1 convolution_convert_fusion.1
  587.9 58.3 %reduce-scatter.16.cloned.1.call-done = bf16[336,128]{1,0:T(8,128)(2,1)} async-done(((bf16[2688,128]{1,0:T(8,128)(2,1)}), bf16[336,128]{1,0:T(8,128)(2,1)}) %reduce-scatter.16.cloned.1.call-update) | async-done | bytes 86032 | tf_op jit(solution)/shard_map/reduce_scatter | solution.py:68
  650.4 124.6 %all-reduce.13.cloned.1.call-done = f32[256,128]{1,0:T(8,128)} async-done(((f32[256,128]{1,0:T(8,128)}), f32[256,128]{1,0:T(8,128)}) %all-reduce.13.cloned.1.call-update) | async-done | bytes 131088
  776.9 16.9 %all-gather.27.cloned.1.call-done = bf16[576,1152]{1,0:T(8,128)(2,1)} async-done(((bf16[144,1152]{1,0:T(8,128)(2,1)}), bf16[576,1152]{1,0:T(8,128)(2,1)}) %all-gather.27.cloned.1.call-update) | async-done | bytes 1327120 | tf_op jit(solution)/shard_map/all_gather | solution.py:64
  795.6 2.6 reshape.257
  799.2 65.4 %reduce-scatter.14.cloned.1.call-done = bf16[144,896]{1,0:T(8,128)(2,1)} async-done(((bf16[1152,896]{1,0:T(8,128)(2,1)}), bf16[144,896]{1,0:T(8,128)(2,1)}) %reduce-scatter.14.cloned.1.call-update) | async-done | bytes 258064 | tf_op jit(solution)/shard_map/reduce_scatter | solution.py:68
  864.6 10.1 %all_gather.46 = bf16[576,896]{1,0:T(8,128)(2,1)S(1)} all-gather(bf16[144,896]{1,0:T(8,128)(2,1)} %reduce-scatter.14.cloned.1.call-done), channel_id=1, replica_groups=mesh['img'=8,'seq'=4] {'seq'}, dimensions={0}, use_global_device_ids=true | all-gather | bytes 1290240 | tf_op jit(solution)/shard_map/all_gather | solution.py:64
  (248 shorter events, 73.9 us)
Async XLA Ops:
  7.2 22.6 %all-gather.29.cloned.1.call-start = ((), (), s32[]{:S(2)}) async-start(), calls=%async_computation.22 | async-start | bytes 1474560 | tf_op jit(solution)/shard_map/all_gather | solution.py:64
  7.9 84.2 %all-gather.13.cloned.1.call-start = ((), (), s32[]{:S(2)}) async-start(), calls=%async_computation.7 | async-start | bytes 2838528 | tf_op jit(solution)/shard_map/all_gather | solution.py:64
  9.5 133.1 %all-gather.15.cloned.1.call-start = ((), (), s32[]{:S(2)}) async-start(), calls=%async_computation.8 | async-start | bytes 2322432 | tf_op jit(solution)/shard_map/all_gather | solution.py:64
  22.5 4.2 copy-start.54
  23.3 9.7 %copy-start.35 = (bf16[896]{0:T(1024)(128)(2,1)}, bf16[896]{0:T(1024)(128)(2,1)S(1)}, u32[]{:S(2)}) copy-start(bf16[896]{0:T(1024)(128)(2,1)S(1)} %pad.59.clone) | copy-start | bytes 5380
  24.3 139.7 %all-gather.19.cloned.1.call-start = ((), (), s32[]{:S(2)}) async-start(), calls=%async_computation.10 | async-start | bytes 1556480 | tf_op jit(solution)/shard_map/all_gather | solution.py:64
  25.2 190.9 %all-gather.23.cloned.1.call-start = ((), (), s32[]{:S(2)}) async-start(), calls=%async_computation.12 | async-start | bytes 2801664 | tf_op jit(solution)/shard_map/all_gather | solution.py:64
  25.3 0.7 collective-permute-start
  26.7 216.9 %all-gather.17.cloned.1.call-start = ((), (), s32[]{:S(2)}) async-start(), calls=%async_computation.9 | async-start | bytes 1474560 | tf_op jit(solution)/shard_map/all_gather | solution.py:188
  31.2 111.4 %copy-start.38 = (f32[512]{0:T(512)}, f32[512]{0:T(512)S(1)}, u32[]{:S(2)}) copy-start(f32[512]{0:T(512)S(1)} %broadcast_multiply_fusion.1) | copy-start | bytes 6148
  33.0 109.7 %copy-start.49 = (f32[512]{0:T(512)}, f32[512]{0:T(512)S(1)}, u32[]{:S(2)}) copy-start(f32[512]{0:T(512)S(1)} %add_rsqrt_fusion.1) | copy-start | bytes 6148
  95.5 50.7 %copy-start.18 = (f32[13536]{0:T(1024)}, f32[13536]{0:T(1024)S(1)}, u32[]{:S(2)}) copy-start(f32[13536]{0:T(1024)S(1)} %reshape.263) | copy-start | bytes 162436
  96.1 50.0 %copy-start.43 = (f32[1152]{0:T(1024)}, f32[1152]{0:T(1024)S(1)}, u32[]{:S(2)}) copy-start(f32[1152]{0:T(1024)S(1)} %get-tuple-element.34) | copy-start | bytes 13828
  163.7 128.1 %all-gather.21.cloned.1.call-start = ((), (), s32[]{:S(2)}) async-start(), calls=%async_computation.11 | async-start | bytes 2985984 | tf_op jit(solution)/shard_map/all_gather | solution.py:64
  179.1 130.4 %all-gather.31.cloned.1.call-start = ((), (), s32[]{:S(2)}) async-start(), calls=%async_computation.23 | async-start | bytes 1474560 | tf_op jit(solution)/shard_map/all_gather | solution.py:64
  179.9 165.5 %reduce-scatter.10.cloned.1.call-start = ((), (), s32[]{:S(2)}) async-start(), calls=%async_computation.14 | async-start | bytes 1474560 | tf_op jit(solution)/shard_map/reduce_scatter | solution.py:68
  236.5 6.4 slice-start
  252.2 39.7 %copy-start.28 = (f32[1152]{0:T(1024)S(1)}, f32[1152]{0:T(1024)}, u32[]{:S(2)}) copy-start(f32[1152]{0:T(1024)} %get-tuple-element.30) | copy-start | bytes 13828
  309.5 7.2 copy-start.51
  319.6 53.8 %reduce-scatter.8.cloned.1.call-start = ((), (), s32[]{:S(2)}) async-start(), calls=%async_computation.13 | async-start | bytes 1474560 | tf_op jit(solution)/shard_map/reduce_scatter | solution.py:68
  325.3 70.3 %all-gather.25.cloned.1.call-start = ((), (), s32[]{:S(2)}) async-start(), calls=%async_computation.15 | async-start | bytes 1474560 | tf_op jit(solution)/shard_map/all_gather | solution.py:64
  376.5 21.2 %copy-start.8 = (bf16[4,512,72]{1,2,0:T(8,128)(2,1)S(1)}, bf16[4,512,72]{1,2,0:T(8,128)(2,1)}, u32[]{:S(2)}) copy-start(bf16[4,512,72]{1,2,0:T(8,128)(2,1)} %convolution_convert_fusion.8) | copy-start | bytes 884740
  376.5 21.3 %copy-start.16 = (bf16[512,288]{0,1:T(8,128)(2,1)S(1)}, bf16[512,288]{0,1:T(8,128)(2,1)}, u32[]{:S(2)}) copy-start(bf16[512,288]{0,1:T(8,128)(2,1)} %copy-done.15) | copy-start | bytes 884740
  376.5 21.3 %copy-start.34 = (f32[4,512]{1,0:T(4,128)S(1)}, f32[4,512]{1,0:T(4,128)}, u32[]{:S(2)}) copy-start(f32[4,512]{1,0:T(4,128)} %copy-done.33) | copy-start | bytes 24580
  376.5 21.3 %copy-start.47 = (pred[512]{0:T(512)(128)(4,1)S(1)}, pred[512]{0:T(512)(128)(4,1)}, u32[]{:S(2)}) copy-start(pred[512]{0:T(512)(128)(4,1)} %fusion.50) | copy-start | bytes 1540
  378.1 66.4 %reduce-scatter.12.cloned.1.call-start = ((), (), s32[]{:S(2)}) async-start(), calls=%async_computation.16 | async-start | bytes 1474560 | tf_op jit(solution)/shard_map/reduce_scatter | solution.py:68
  397.8 3.9 copy-start.10
  408.7 101.3 %reduce-scatter.18.cloned.1.call-start = ((), (), s32[]{:S(2)}) async-start(), calls=%async_computation.19 | async-start | bytes 2985984 | tf_op jit(solution)/shard_map/reduce_scatter | solution.py:68
  413.4 169.5 %reduce-scatter.20.cloned.1.call-start = ((), (), s32[]{:S(2)}) async-start(), calls=%async_computation.21 | async-start | bytes 2801664 | tf_op jit(solution)/shard_map/reduce_scatter | solution.py:68
  438.7 207.4 %reduce-scatter.16.cloned.1.call-start = ((), (), s32[]{:S(2)}) async-start(), calls=%async_computation.18 | async-start | bytes 774144 | tf_op jit(solution)/shard_map/reduce_scatter | solution.py:68
  441.7 4.0 copy-start.29
  441.8 4.0 copy-start.30
  441.8 4.0 copy-start.31
  441.8 4.0 copy-start.32
  441.8 142.9 %copy-start.23 = (bf16[512,4,72]{0,2,1:T(8,128)(2,1)S(1)}, bf16[512,4,72]{0,2,1:T(8,128)(2,1)}, u32[]{:S(2)}) copy-start(bf16[512,4,72]{0,2,1:T(8,128)(2,1)} %copy-done.22) | copy-start | bytes 884740
  441.8 142.9 %copy-start.25 = (bf16[512,4,72]{0,2,1:T(8,128)(2,1)S(1)}, bf16[512,4,72]{0,2,1:T(8,128)(2,1)}, u32[]{:S(2)}) copy-start(bf16[512,4,72]{0,2,1:T(8,128)(2,1)} %copy-done.24) | copy-start | bytes 884740
  441.9 142.9 %copy-start.27 = (bf16[4,512,72]{1,2,0:T(8,128)(2,1)S(1)}, bf16[4,512,72]{1,2,0:T(8,128)(2,1)}, u32[]{:S(2)}) copy-start(bf16[4,512,72]{1,2,0:T(8,128)(2,1)} %copy-done.26) | copy-start | bytes 884740
  441.9 142.9 %copy-start.37 = (bf16[896]{0:T(1024)(128)(2,1)S(1)}, bf16[896]{0:T(1024)(128)(2,1)}, u32[]{:S(2)}) copy-start(bf16[896]{0:T(1024)(128)(2,1)} %copy-done.35) | copy-start | bytes 5380
  441.9 142.9 %copy-start.39 = (f32[512]{0:T(512)S(1)}, f32[512]{0:T(512)}, u32[]{:S(2)}) copy-start(f32[512]{0:T(512)} %copy-done.38) | copy-start | bytes 6148
  441.9 142.9 %copy-start.44 = (f32[1152]{0:T(1024)S(1)}, f32[1152]{0:T(1024)}, u32[]{:S(2)}) copy-start(f32[1152]{0:T(1024)} %copy-done.43) | copy-start | bytes 13828
  441.9 142.9 %copy-start.50 = (f32[512]{0:T(512)S(1)}, f32[512]{0:T(512)}, u32[]{:S(2)}) copy-start(f32[512]{0:T(512)} %copy-done.49) | copy-start | bytes 6148
  443.1 331.9 %all-reduce.13.cloned.1.call-start = ((), (), s32[]{:S(2)}) async-start(), calls=%async_computation.24 | async-start | bytes 262144
  446.9 346.9 %all-gather.27.cloned.1.call-start = ((), (), s32[]{:S(2)}) async-start(), calls=%async_computation.20 | async-start | bytes 1658880 | tf_op jit(solution)/shard_map/all_gather | solution.py:64
  510.0 354.6 %reduce-scatter.14.cloned.1.call-start = ((), (), s32[]{:S(2)}) async-start(), calls=%async_computation.17 | async-start | bytes 2322432 | tf_op jit(solution)/shard_map/reduce_scatter | solution.py:68
  582.9 64.9 %collective-permute-start.2 = (bf16[1216,128]{1,0:T(8,128)(2,1)}, bf16[1216,128]{1,0:T(8,128)(2,1)S(1)}, u32[]{:S(2)}, u32[]{:S(2)}) collective-permute-start(bf16[1216,128]{1,0:T(8,128)(2,1)} %reduce-scatter.20.cloned.1.call-done), channel_id=1, source_target_pairs={{0,0},{4,1},{8,2},{12,3},{16,4},{20,5},{24,6},{28,7},{1,8},{5,9},{... | collective-permute-start | bytes 933896 | tf_op jit(solution)/shard_map/ppermute | solution.py:248
  587.9 61.4 %copy-start.7 = (f32[128,1152]{1,0:T(8,128)S(1)}, f32[128,1152]{1,0:T(8,128)}, u32[]{:S(2)}) copy-start(f32[128,1152]{1,0:T(8,128)} %copy-done.6) | copy-start | bytes 1769476
  587.9 61.4 %copy-start.17 = (bf16[128,1152]{1,0:T(8,128)(2,1)S(1)}, bf16[128,1152]{1,0:T(8,128)(2,1)}, u32[]{:S(2)}) copy-start(bf16[128,1152]{1,0:T(8,128)(2,1)} %reduce-scatter.12.cloned.1.call-done) | copy-start | bytes 884740
  646.2 2.4 collective-permute-start.1
  (30 other events, 53.4 us)
Sparse Core Ops, SparseCore 0:
  9.5 20.1 all-gather.28
  33.2 58.9 all-gather.12
  94.9 47.6 all-gather.14
  144.6 16.3 all-gather.18
  163.1 52.9 all-gather.22
  218.1 15.9 all-gather.16
  236.8 54.9 all-gather.20
  293.4 15.9 all-gather.30
  319.7 25.6 reduce-scatter.9
  347.8 25.6 reduce-scatter.7
  378.2 17.4 all-gather.24
  408.9 25.6 reduce-scatter.11
  438.2 71.8 reduce-scatter.17
  513.4 69.4 reduce-scatter.19
  586.0 60.1 reduce-scatter.15
  651.6 123.3 all-reduce.12
  776.4 17.2 all-gather.26
  797.2 67.4 reduce-scatter.13

commit v2 on v1

--- a/solution.py
+++ b/solution.py
@@ -121,10 +121,15 @@
     def mine(values):
         return lax.dynamic_slice_in_dim(values, position * slot, slot)
 
-    qkv_seq = unpack_blocks(gather(pack(w_qkv), "seq"), seq_count, shard_qkv)
-    out_vec = gather(pack(jnp.concatenate([w_out, vectors])), both)
+    shard_ov = shard_out + shard_vec
+    local = gather(pack(jnp.concatenate([w_qkv, w_fc1, w_out, vectors])), "seq")
+    local = local.reshape(seq_count, -1)
     x_all16 = gather(tokens[0], "seq")
-    qkv_rows = qkv_seq.reshape(rows, 3 * width)
+    qkv_rows = local[:, :shard_qkv].reshape(rows, 3 * width)
+    fc1_rows = local[:, shard_qkv : shard_qkv + shard_fc1].reshape(rows, hidden)
+    ov_flat = local[:, shard_qkv + shard_fc1 : shard_qkv + shard_fc1 + shard_ov].reshape(-1)
+    ov_cols = round_up(-(-ov_flat.shape[0] // rows), LANES)
+    ov_part = jnp.pad(ov_flat, (0, rows * ov_cols - ov_flat.shape[0])).reshape(rows, ov_cols)
     qkv_part = jnp.concatenate(
         [
             lax.dynamic_slice_in_dim(qkv_rows, j * width + position * cols, cols, axis=1)
@@ -133,20 +138,22 @@
         + [jnp.zeros((rows, pad_cols), bf16)],
         axis=1,
     )
-    mat_qkv = gather(qkv_part, "img")
-    fc1_seq = unpack_blocks(gather(pack(w_fc1), "seq"), seq_count, shard_fc1)
     fc1_part = jnp.pad(
-        lax.dynamic_slice_in_dim(
-            fc1_seq.reshape(rows, hidden), position * units, units, axis=1
-        ),
+        lax.dynamic_slice_in_dim(fc1_rows, position * units, units, axis=1),
         ((0, 0), (0, pad_units)),
     )
-    mat_fc1 = gather(fc1_part, "img")
-    fc2_chunk = lax.ppermute(pack(w_fc2), both, to_quarter)
+    fc2_chunk = lax.ppermute(pack(w_fc2), both, to_quarter).reshape(-1)[:shard_fc2]
+    fc2_part = jnp.pad(fc2_chunk.reshape(rows, units), ((0, 0), (0, pad_units)))
+    weights = gather(jnp.concatenate([qkv_part, fc1_part, fc2_part, ov_part], axis=1), "img")
+    end_qkv = 3 * cols + pad_cols
+    end_fc1 = end_qkv + units + pad_units
+    end_fc2 = end_fc1 + units + pad_units
+    mat_qkv = weights[:, :end_qkv]
+    mat_fc1 = weights[:, end_qkv:end_fc1]
     mat_fc2 = jnp.pad(
-        unpack_blocks(gather(fc2_chunk, "img"), img_count, shard_fc2).reshape(units, width),
-        ((0, pad_units), (0, 0)),
-    )
+        weights[:, end_fc1 : end_fc1 + units].reshape(units, width), ((0, pad_units), (0, 0))
+    )
+    out_vec = weights[:, end_fc2:].reshape(img_count, -1)[:, : seq_count * shard_ov]
     cot_all = gather(cotangent[0], "seq")
 
     blocks_ov = out_vec.reshape(device_count, -1)
@@ -205,13 +212,8 @@
     grad_resid = grad_y + norm_back(grad_ln2, normed2_mine, mine(rstd2), gain2)
     grad_resid16 = gather(grad_resid.astype(bf16), "seq")
 
-    def reduce_rows(partial):
-        return scatter_sum(partial, "img")
-
-    sum_fc1 = reduce_rows(weight_grad(ln2, grad_pre16))
-    sum_fc2 = reduce_rows(
-        pack_blocks(weight_grad(act, grad_y16)[:units].reshape(-1), img_count)
-    )
+    part_fc1 = weight_grad(ln2, grad_pre16)
+    part_fc2 = pack_blocks(weight_grad(act, grad_y16)[:units].reshape(-1), img_count)
     out_terms = scatter_sum(
         jnp.dot(act, mat_fc2, preferred_element_type=f32).astype(bf16), "seq"
     ).astype(f32)
@@ -232,25 +234,10 @@
         axis=1,
     )
     grad_ln1 = scatter_sum(dot_t(grad_qkv16, mat_qkv).astype(bf16), "seq").astype(f32)
-    sum_qkv = reduce_rows(weight_grad(ln1, grad_qkv16))
-    sum_out = reduce_rows(
-        pack_blocks(weight_grad(mixed_mine, grad_resid16).reshape(-1), img_count)
-    )
+    part_qkv = weight_grad(ln1, grad_qkv16)
+    part_out = pack_blocks(weight_grad(mixed_mine, grad_resid16).reshape(-1), img_count)
     normed1_mine, rstd1_mine = normalize(tokens[0].astype(f32))
     input_grad = grad_resid + norm_back(grad_ln1, normed1_mine, rstd1_mine, gain1)
-
-    def own_block(rows_sum, thirds, used, size):
-        blocks = gather(rows_sum, "seq").reshape(seq_count, rows, -1)[:, :, : thirds * used]
-        whole = blocks.reshape(seq_count, rows, thirds, used).transpose(1, 2, 0, 3)
-        return lax.dynamic_slice_in_dim(whole.reshape(-1), position * size, size).astype(f32)
-
-    def own_chunk(packed, size):
-        return lax.ppermute(packed, both, to_owner).reshape(-1)[:size].astype(f32)
-
-    grad_fc1 = own_block(sum_fc1, 1, units, shard_fc1)
-    grad_fc2 = own_chunk(sum_fc2, shard_fc2)
-    grad_qkv = own_block(sum_qkv, 3, cols, shard_qkv)
-    grad_out = own_chunk(sum_out, shard_out)
 
     def spread(part, full):
         return lax.dynamic_update_slice_in_dim(
@@ -277,8 +264,30 @@
     g_vec = jnp.concatenate(
         [g_front.reshape(device_count, -1), g_rest.reshape(device_count, -1)], axis=1
     )
-    g_vec = jnp.pad(g_vec, ((0, 0), (0, round_up(shard_vec, 1024) - shard_vec)))
-    vec_mine = scatter_sum(g_vec.reshape(-1, LANES), both).reshape(-1)
+    vec_pad = round_up(shard_vec, 4 * LANES)
+    part_vec = jnp.pad(g_vec, ((0, 0), (0, vec_pad - shard_vec))).astype(bf16)
+
+    parts = [
+        part.reshape(img_count, -1, LANES)
+        for part in (part_qkv, part_fc1, part_vec, part_fc2, part_out)
+    ]
+    sizes = [part.shape[1] for part in parts]
+    summed = scatter_sum(jnp.concatenate(parts, axis=1).reshape(-1, LANES), "img")
+    ends = [sum(sizes[: i + 1]) for i in range(5)]
+    chunks = lax.ppermute(summed[ends[2] :], both, to_owner)
+    grad_fc2 = chunks[: sizes[3]].reshape(-1)[:shard_fc2].astype(f32)
+    grad_out = chunks[sizes[3] :].reshape(-1)[:shard_out].astype(f32)
+    shared = gather(summed[: ends[2]], "seq").reshape(seq_count, ends[2], LANES)
+
+    def own_block(packed, thirds, used, size):
+        blocks = packed.reshape(seq_count, rows, -1)[:, :, : thirds * used]
+        whole = blocks.reshape(seq_count, rows, thirds, used).transpose(1, 2, 0, 3)
+        return lax.dynamic_slice_in_dim(whole.reshape(-1), position * size, size).astype(f32)
+
+    grad_qkv = own_block(shared[:, : ends[0]], 3, cols, shard_qkv)
+    grad_fc1 = own_block(shared[:, ends[0] : ends[1]], 1, units, shard_fc1)
+    vec_sums = jnp.sum(shared[:, ends[1] :].astype(f32), axis=0).reshape(seq_count, vec_pad)
+    vec_mine = lax.dynamic_slice_in_dim(vec_sums, position, 1).reshape(-1)
     return (
         output[None],
         input_grad[None],

time: 897 us -> 679 us (0.76)
  waiting for transfers between devices: 657 us -> 410 us
  local copies, waits for them, and re-layouts: 108 us -> 155 us
  blocking collectives: 21.3 us -> 0 us
    unnamed x19 -> x11, waiting for transfers between devices: 126 us -> 1.38 us
    reduce_scatter x7 -> x4, waiting for transfers between devices: 303 us -> 184 us  [scatter_sum(): return lax.psum_scatter(value, axes, scatter_dimension=0, tiled=True)]
    all_gather x2 -> x0, blocking collectives: 21.3 us -> none  [gather(): return lax.all_gather(value, axes, axis=0, tiled=True)]
    reshape x7 -> x15, local copies, waits for them, and re-layouts: 14.2 us -> 30.3 us  [the longest x3 9.87 us: shards(): part.reshape(img_count, -1, LANES)]
    concatenate x1 -> x4, local copies, waits for them, and re-layouts: 0.08 us -> 13.9 us  [the longest x1 10.4 us: shards(): local = gather(pack(jnp.concatenate([w_qkv, w_fc1, w_out, vectors])), 'seq')]
    unnamed x118 -> x114, local copies, waits for them, and re-layouts: 29.4 us -> 42.5 us
    another operation x7 -> x4, local copies, waits for them, and re-layouts: 11.7 us -> 0.59 us  [the longest x1 5.95 us: shards(): unpack_blocks(gather(fc2_chunk, 'img'), img_count, shard_fc2)]
    all_gather x9 -> x6, waiting for transfers between devices: 228 us -> 224 us  [gather(): return lax.all_gather(value, axes, axis=0, tiled=True)]
  transfers between devices with their start and end apart: 21 -> 13, of which waited for: 15 -> 8; matrix products, arithmetic and copies ran while one was open for 17% -> 19% of each run, Pallas kernels for 0% -> 0%
where the time goes in v2:
time: 679 us; the launch traced here: 670 us
  waiting for transfers between devices  410 us (60%)
  local copies, waits for them, and re-layouts  155 us (23%)
  matrix products  61.4 us (9%)
  other arithmetic  27.3 us (4%)
  between operations  15.2 us (2%)
    all_gather x6, waiting for transfers between devices, gather(): return lax.all_gather(value, axes, axis=0, tiled=True)  224 us
    reduce_scatter x4, waiting for transfers between devices, scatter_sum(): return lax.psum_scatter(value, axes, scatter_dimension=0, tiled=True)  184 us
    unnamed x114, local copies, waits for them, and re-layouts  42.5 us
    dot_general x4, matrix products, dot_t(): lax.dot_general(left, right, (((1,), (1,)), ((), ())), preferred_element_...  17.1 us
    dot_general x4, matrix products, weight_grad(): lax.dot_general(left, right, (((0,), (0,)), ((), ())), preferred_element_...  16 us
  transfers between devices with their start and end apart: 13, of which 8 were waited for; matrix products, arithmetic and copies ran while one was open for 19% of the time, Pallas kernels for 0%

profile of v2, /device:TPU:0, one launch (start us, length us, event | category | flops | bytes accessed | tf_op | source)
XLA Modules:
  0.0 670.3 jit_solution(507022705305518858)
XLA Ops:
  7.2 10.4 %concatenate.29 = bf16[321255]{0:T(1024)(128)(2,1)S(1)} concatenate(bf16[124416]{0:T(1024)(128)(2,1)} %param.10, bf16[154944]{0:T(1024)(128)(2,1)} %param.12, bf16[41472]{0:T(1024)(128)(2,1)} %param.11, bf16[423]{0:T(512)(128)(2,1)} %param.14), dimensions={0} | concatenate | bytes 1285020 | tf_op jit(solution)/shard_map/concatenate | solution.py:125
  21.4 33.0 %all-gather.10.cloned.1.call-done = bf16[10048,128]{1,0:T(8,128)(2,1)} async-done(((bf16[2512,128]{1,0:T(8,128)(2,1)}), bf16[10048,128]{1,0:T(8,128)(2,1)}) %all-gather.10.cloned.1.call-update) | async-done | bytes 2572304 | tf_op jit(solution)/shard_map/all_gather | solution.py:64
  54.4 2.7 reshape.261
  64.2 2.0 reshape.263
  71.1 3.9 all-gather.20.cloned.1.call-done
  78.3 147.5 %all-gather.12.cloned.1.call-done = bf16[1152,4480]{1,0:T(8,128)(2,1)} async-done(((bf16[144,4480]{1,0:T(8,128)(2,1)}), bf16[1152,4480]{1,0:T(8,128)(2,1)}) %all-gather.12.cloned.1.call-update) | async-done | bytes 10321936 | tf_op jit(solution)/shard_map/all_gather | solution.py:64
  227.6 3.0 reshape.269
  232.4 4.9 reshape.305
  237.3 5.4 reshape.270
  244.1 3.5 fusion.20
  249.7 2.2 copy.61
  265.5 6.4 reshape.276
  273.7 6.6 reshape.303
  280.3 5.9 reshape.277
  286.9 3.5 reshape.274
  290.6 3.8 fusion.70
  296.5 5.1 convolution_add_fusion
  301.6 6.0 fusion.71
  308.7 4.6 convolution_convert_fusion.3
  313.4 5.6 convolution_convert_fusion.4
  320.4 16.9 %reduce-scatter.7.cloned.1.call-done = bf16[128,1152]{1,0:T(8,128)(2,1)} async-done(((bf16[512,1152]{1,0:T(8,128)(2,1)}), bf16[128,1152]{1,0:T(8,128)(2,1)}) %reduce-scatter.7.cloned.1.call-update) | async-done | bytes 294928 | tf_op jit(solution)/shard_map/reduce_scatter | solution.py:68
  337.3 2.0 fusion.33
  339.8 25.7 %reduce-scatter.5.cloned.1.call-done = bf16[128,1152]{1,0:T(8,128)(2,1)} async-done(((bf16[512,1152]{1,0:T(8,128)(2,1)}), bf16[128,1152]{1,0:T(8,128)(2,1)}) %reduce-scatter.5.cloned.1.call-update) | async-done | bytes 294928 | tf_op jit(solution)/shard_map/reduce_scatter | solution.py:68
  365.5 2.9 fusion.64
  372.4 14.4 %all-gather.16.cloned.1.call-done = bf16[512,1152]{1,0:T(8,128)(2,1)} async-done(((bf16[128,1152]{1,0:T(8,128)(2,1)}), bf16[512,1152]{1,0:T(8,128)(2,1)}) %all-gather.16.cloned.1.call-update) | async-done | bytes 1179664 | tf_op jit(solution)/shard_map/all_gather | solution.py:64
  386.8 2.0 convolution_convert_fusion.6
  389.0 3.9 multiply_convert_fusion
  397.0 4.5 convolution_convert_fusion.2
  401.6 4.5 convolution_convert_fusion
  406.2 5.2 reshape.280
  411.3 4.0 fusion.48
  417.0 5.8 reshape.307
  422.9 5.0 reshape_reshape.12
  427.9 3.3 pad_bitcast_fusion
  436.2 4.6 convolution_convert_fusion.1
  440.9 4.7 reshape.279
  445.5 2.8 convolution_convert_fusion.5
  448.4 3.0 reshape_reshape.14
  451.8 2.0 pad_bitcast_fusion.1
  453.8 3.3 constant_dynamic-update-slice_fusion.2
  460.3 2.8 concatenate.35
  465.9 3.6 bitcast_dynamic-update-slice_fusion
  470.5 141.6 %reduce-scatter.11.cloned.1.call-done = bf16[3872,128]{1,0:T(8,128)(2,1)} async-done(((bf16[30976,128]{1,0:T(8,128)(2,1)}), bf16[3872,128]{1,0:T(8,128)(2,1)}) %reduce-scatter.11.cloned.1.call-update) | async-done | bytes 991248 | tf_op jit(solution)/shard_map/reduce_scatter | solution.py:68
  617.6 25.3 %all-gather.18.cloned.1.call-done = bf16[9280,128]{1,0:T(8,128)(2,1)} async-done(((bf16[2320,128]{1,0:T(8,128)(2,1)}), bf16[9280,128]{1,0:T(8,128)(2,1)}) %all-gather.18.cloned.1.call-update) | async-done | bytes 2375696 | tf_op jit(solution)/shard_map/all_gather | solution.py:64
  644.3 2.3 slice.186
  649.5 3.7 reshape.290
  657.2 2.0 reshape.287
  660.4 2.0 dynamic-slice_convert_fusion
  (241 shorter events, 85.2 us)
Async XLA Ops:
  7.2 12.1 %copy-start.23 = (bf16[154944]{0:T(1024)(128)(2,1)S(1)}, bf16[154944]{0:T(1024)(128)(2,1)}, u32[]{:S(2)}) copy-start(bf16[154944]{0:T(1024)(128)(2,1)} %param.13) | copy-start | bytes 929668
  7.2 47.3 %all-gather.10.cloned.1.call-start = ((), (), s32[]{:S(2)}) async-start(), calls=%async_computation.4 | async-start | bytes 3215360 | tf_op jit(solution)/shard_map/all_gather | solution.py:64
  18.5 56.6 %all-gather.20.cloned.1.call-start = ((), (), s32[]{:S(2)}) async-start(), calls=%async_computation.13 | async-start | bytes 1474560 | tf_op jit(solution)/shard_map/all_gather | solution.py:64
  19.3 206.5 %all-gather.12.cloned.1.call-start = ((), (), s32[]{:S(2)}) async-start(), calls=%async_computation.5 | async-start | bytes 11612160 | tf_op jit(solution)/shard_map/all_gather | solution.py:64
  19.3 0.7 collective-permute-start
  66.1 2.3 copy-start.17
  68.2 2.4 copy-start.49
  70.3 216.6 %all-gather.14.cloned.1.call-start = ((), (), s32[]{:S(2)}) async-start(), calls=%async_computation.6 | async-start | bytes 1474560 | tf_op jit(solution)/shard_map/all_gather | solution.py:195
  76.6 166.9 %copy-start.33 = (f32[512]{0:T(512)}, f32[512]{0:T(512)S(1)}, u32[]{:S(2)}) copy-start(f32[512]{0:T(512)S(1)} %broadcast_multiply_fusion.1) | copy-start | bytes 6148
  78.3 165.2 %copy-start.47 = (f32[512]{0:T(512)}, f32[512]{0:T(512)S(1)}, u32[]{:S(2)}) copy-start(f32[512]{0:T(512)S(1)} %add_rsqrt_fusion.1) | copy-start | bytes 6148
  242.8 22.7 %copy-start.22 = (f32[13536]{0:T(1024)}, f32[13536]{0:T(1024)S(1)}, u32[]{:S(2)}) copy-start(f32[13536]{0:T(1024)S(1)} %reshape.293) | copy-start | bytes 162436
  254.9 3.2 copy-start.11
  258.1 2.1 copy-start
  260.7 2.5 copy-start.18
  263.2 38.4 %all-gather.22.cloned.1.call-start = ((), (), s32[]{:S(2)}) async-start(), calls=%async_computation.14 | async-start | bytes 1474560 | tf_op jit(solution)/shard_map/all_gather | solution.py:64
  263.8 73.5 %reduce-scatter.7.cloned.1.call-start = ((), (), s32[]{:S(2)}) async-start(), calls=%async_computation.8 | async-start | bytes 1474560 | tf_op jit(solution)/shard_map/reduce_scatter | solution.py:68
  265.5 6.4 slice-start.3
  286.9 3.7 copy-start.3
  296.5 5.1 copy-start.39
  313.3 52.2 %copy-start.20 = (bf16[1,128,1152]{2,1,0:T(8,128)(2,1)S(1)}, bf16[1,128,1152]{2,1,0:T(8,128)(2,1)}, u32[]{:S(2)}) copy-start(bf16[1,128,1152]{2,1,0:T(8,128)(2,1)} %param.15) | copy-start | bytes 884740
  313.3 52.2 %reduce-scatter.5.cloned.1.call-start = ((), (), s32[]{:S(2)}) async-start(), calls=%async_computation.7 | async-start | bytes 1474560 | tf_op jit(solution)/shard_map/reduce_scatter | solution.py:68
  319.1 67.8 %all-gather.16.cloned.1.call-start = ((), (), s32[]{:S(2)}) async-start(), calls=%async_computation.9 | async-start | bytes 1474560 | tf_op jit(solution)/shard_map/all_gather | solution.py:64
  320.4 49.6 %copy-start.4 = (bf16[1,128,1152]{2,1,0:T(8,128)(2,1)S(1)}, bf16[1,128,1152]{2,1,0:T(8,128)(2,1)}, u32[]{:S(2)}) copy-start(bf16[1,128,1152]{2,1,0:T(8,128)(2,1)} %param.8) | copy-start | bytes 884740
  368.5 20.4 %copy-start.8 = (bf16[4,512,72]{1,2,0:T(8,128)(2,1)S(1)}, bf16[4,512,72]{1,2,0:T(8,128)(2,1)}, u32[]{:S(2)}) copy-start(bf16[4,512,72]{1,2,0:T(8,128)(2,1)} %convolution_convert_fusion.8) | copy-start | bytes 884740
  368.5 20.5 %copy-start.19 = (bf16[512,288]{0,1:T(8,128)(2,1)S(1)}, bf16[512,288]{0,1:T(8,128)(2,1)}, u32[]{:S(2)}) copy-start(bf16[512,288]{0,1:T(8,128)(2,1)} %copy-done.18) | copy-start | bytes 884740
  368.5 20.5 %copy-start.29 = (f32[4,512]{1,0:T(4,128)S(1)}, f32[4,512]{1,0:T(4,128)}, u32[]{:S(2)}) copy-start(f32[4,512]{1,0:T(4,128)} %copy-done.28) | copy-start | bytes 24580
  368.5 20.5 %copy-start.40 = (pred[512]{0:T(512)(128)(4,1)S(1)}, pred[512]{0:T(512)(128)(4,1)}, u32[]{:S(2)}) copy-start(pred[512]{0:T(512)(128)(4,1)} %fusion.57) | copy-start | bytes 1540
  369.2 89.8 %reduce-scatter.9.cloned.1.call-start = ((), (), s32[]{:S(2)}) async-start(), calls=%async_computation.10 | async-start | bytes 1474560 | tf_op jit(solution)/shard_map/reduce_scatter | solution.py:68
  370.1 18.8 %copy-start.42 = (f32[128]{0:T(128)}, f32[128]{0:T(128)S(1)}, u32[]{:S(2)}) copy-start(f32[128]{0:T(128)S(1)} %broadcast_multiply_fusion.4) | copy-start | bytes 1540
  389.0 3.9 copy-start.12
  394.1 2.2 copy-start.24
  394.1 2.9 copy-start.46
  397.0 4.6 copy-start.6
  401.6 210.6 %reduce-scatter.11.cloned.1.call-start = ((), (), s32[]{:S(2)}) async-start(), calls=%async_computation.11 | async-start | bytes 8921088 | tf_op jit(solution)/shard_map/reduce_scatter | solution.py:68
  406.2 5.2 copy-start.41
  427.9 4.9 copy-start.44
  427.9 8.4 %copy-start.34 = (f32[512]{0:T(512)S(1)}, f32[512]{0:T(512)}, u32[]{:S(2)}) copy-start(f32[512]{0:T(512)} %copy-done.33) | copy-start | bytes 6148
  445.5 5.8 copy-start.45
  457.1 3.2 copy-start.30
  457.1 3.2 copy-start.31
  465.9 3.6 copy-start.10
  470.4 143.6 %copy-start.15 = (bf16[128,1152]{1,0:T(8,128)(2,1)S(1)}, bf16[128,1152]{1,0:T(8,128)(2,1)}, u32[]{:S(2)}) copy-start(bf16[128,1152]{1,0:T(8,128)(2,1)} %reduce-scatter.9.cloned.1.call-done) | copy-start | bytes 884740
  470.4 143.6 %copy-start.43 = (f32[128]{0:T(128)S(1)}, f32[128]{0:T(128)}, u32[]{:S(2)}) copy-start(f32[128]{0:T(128)} %copy-done.42) | copy-start | bytes 1540
  470.4 143.6 %copy-start.48 = (f32[128]{0:T(128)S(1)}, f32[128]{0:T(128)}, u32[]{:S(2)}) copy-start(f32[128]{0:T(128)} %add_rsqrt_fusion.2) | copy-start | bytes 1540
  470.5 172.4 %all-gather.18.cloned.1.call-start = ((), (), s32[]{:S(2)}) async-start(), calls=%async_computation.12 | async-start | bytes 2969600 | tf_op jit(solution)/shard_map/all_gather | solution.py:64
  612.2 2.9 copy-start.21
  613.3 2.7 collective-permute-start.1
  649.0 4.2 copy-start.9
  (20 other events, 30.1 us)
Sparse Core Ops, SparseCore 0:
  18.6 35.7 all-gather.9
  56.0 19.0 all-gather.19
  77.2 148.5 all-gather.11
  263.3 15.5 all-gather.13
  280.3 17.4 all-gather.21
  313.5 23.8 reduce-scatter.6
  339.9 25.6 reduce-scatter.4
  369.4 17.4 all-gather.15
  401.7 25.6 reduce-scatter.8
  470.6 141.5 reduce-scatter.10
  616.1 26.7 all-gather.17
